TPU v7x, 32 devices: a whole 2x2x4 slice. The times are simulated.
32 devices in a mesh: replica: 8 (over z, y), fsdp: 4 (over x, core).
Axes of the slice: x: 2, y: 2, z: 4, core: 2. Of those that a mesh axis runs over, the one named last changes fastest.
Arguments:
- inner_weights: bfloat16 [8, 4, 1024, 8192], P('replica', None, 'fsdp'), may hold values from -6 to 6
- snapshot: bfloat16 [1024, 8192], P('fsdp'), may hold values from -6 to 6
- momentum: float32 [1024, 8192], P('fsdp', 'replica'), may hold values from -6 to 6
- rand_bits: int32 [8, 1024, 8192], P('replica', 'fsdp'), may hold values from 0 to 4095
- fragment: int32 [1], replicated, may hold values from 0 to 3
Outputs:
- new_snapshot: bfloat16 [1024, 8192], P('fsdp')
- new_momentum: float32 [1024, 8192], P('fsdp', 'replica')
- new_inner: bfloat16 [8, 4, 1024, 8192], P('replica', None, 'fsdp')
Inputs may be any that keep to these rules, and one draw needn't show every extreme that they name: fragment[0] is one of 0, 1, 2, 3, the fragment of the window that syncs.
All inputs are finite; a program needn't handle non-finite values.
Results may differ from a plain program's by a relative error of at most 0.0075.
Values may be sent and summed in bfloat16 or wider, within the bound.
A program may use at most 128 MiB of HBM per device.

v0:
```python
import functools

import jax
import jax.numpy as jnp
from jax import lax
from jax.experimental import pallas as pl
from jax.experimental.pallas import tpu as pltpu
from jax.sharding import PartitionSpec as P

momentum_coef = 0.9
outer_rate = 0.7
blend_keep = 0.5
grid_scale = 4.0
bit_levels = 4096.0
MESH = pl.DeviceIdType.MESH
CHUNK_ROWS = 32
OLDEST_FIRST = True
EXCHANGE_VMEM = 42 << 20
FINISH_VMEM = 10 << 20


def when(cond):
    if isinstance(cond, bool):
        return (lambda f: f()) if cond else (lambda f: None)
    return pl.when(cond)


def grid_of(n):
    inner = max(k for k in range(1, n + 1) if n % k == 0 and k * k <= n)
    return n // inner, inner


class Part:
    def __init__(self, bufs, sems, line1, line2, me, cols, width, draining):
        self.own, self.r1, self.l1, self.r2, self.l2, self.res = bufs
        (self.s1, self.sr1, self.sl1, self.s2, self.sr2, self.sl2,
         self.g2, self.g2r, self.g2l, self.g1, self.g1r, self.g1l) = sems
        (self.p1, self.n1, self.d1) = line1
        (self.p2, self.n2, self.d2) = line2
        self.me, self.cols, self.width = me, cols, width
        self.top = self.n1 + self.n2 - 2
        self.last = 2 * self.top
        self.draining = draining

    def send(self, src, dst, send_sem, recv_sem, delta):
        copy = pltpu.make_async_remote_copy(
            src_ref=src, dst_ref=dst, send_sem=send_sem, recv_sem=recv_sem,
            device_id={"replica": self.me + delta}, device_id_type=MESH,
        )
        if self.draining:
            copy.wait_send()
        else:
            copy.start()

    def arrive(self, dst, recv_sem):
        if not self.draining:
            pltpu.make_async_remote_copy(
                src_ref=dst, dst_ref=dst, send_sem=recv_sem, recv_sem=recv_sem,
                device_id={"replica": self.me}, device_id_type=MESH,
            ).wait_recv()

    def add1(self, c, q, recv):
        if not self.draining:
            for i in range(self.n2):
                self.own[c, q, i] = self.own[c, q, i] + recv[c, q, i]

    def add2(self, c, q, recv):
        if not self.draining:
            self.own[c, self.p1, q] = self.own[c, self.p1, q] + recv[c, q]

    def send1(self, c, q, right):
        recv, sem, delta = (self.r1, self.sr1, self.d1) if right else (self.l1, self.sl1, -self.d1)
        self.send(self.own.at[c, q], recv.at[c, q], self.s1.at[c, q], sem.at[c, q], delta)

    def send2(self, c, q, right):
        recv, sem, delta = (self.r2, self.sr2, self.d2) if right else (self.l2, self.sl2, -self.d2)
        self.send(self.own.at[c, self.p1, q], recv.at[c, q], self.s2.at[c, q], sem.at[c, q], delta)

    def gsend2(self, c, q, right):
        sem, delta = (self.g2r, self.d2) if right else (self.g2l, -self.d2)
        block = self.res.at[c, self.p1, q]
        self.send(block, block, sem.at[c, q], self.g2.at[c, q], delta)

    def gsend1(self, c, q1, q2, right):
        sem, delta = (self.g1r, self.d1) if right else (self.g1l, -self.d1)
        block = self.res.at[c, q1, q2]
        self.send(block, block, sem.at[c, q1, q2], self.g1.at[c, q1, q2], delta)

    def spread1(self, c, q2):
        p1 = self.p1
        when(p1 < self.n1 - 1)(lambda: self.gsend1(c, p1, q2, True))
        when(p1 > 0)(lambda: self.gsend1(c, p1, q2, False))

    def reduce_line(self, c, h, p, n, send, arrived, recvs, sems, add):
        right_recv, left_recv = recvs
        right_sem, left_sem = sems

        @when(p == h)
        def _():
            for q in range(n - 1, h - (h > 0), -1):
                if h > 0:
                    self.arrive(right_recv.at[c, q], right_sem.at[c, q])
                    if q > h or arrived:
                        add(c, q, right_recv)
                if q > h:
                    send(c, q, True)

        e = n - 1 - h

        @when(p == e)
        def _():
            for q in range(0, e + (h > 0)):
                if h > 0:
                    self.arrive(left_recv.at[c, q], left_sem.at[c, q])
                    if q < e or arrived:
                        add(c, q, left_recv)
                if q < e:
                    send(c, q, False)

    def hop1(self, s, c):
        if s < self.n1:
            self.reduce_line(c, s, self.p1, self.n1, self.send1, True, (self.r1, self.l1), (self.sr1, self.sl1), self.add1)

    def hop2(self, s, c):
        h = s - (self.n1 - 1)
        if 0 <= h < self.n2:
            self.reduce_line(c, h, self.p2, self.n2, self.send2, False, (self.r2, self.l2), (self.sr2, self.sl2), self.add2)

    def update(self, c, snap, mom, mom_next, acc, replicas, share):
        p1, p2 = self.p1, self.p2
        if not self.draining:
            acc[...] = self.own[c, p1, p2].astype(jnp.float32)

            @when(p2 > 0)
            def _():
                acc[...] += self.r2[c, p2].astype(jnp.float32)

            @when(p2 < self.n2 - 1)
            def _():
                acc[...] += self.l2[c, p2].astype(jnp.float32)

            start = self.me * share + self.cols
            if not isinstance(start, int):
                start = pl.multiple_of(start, 128)
            here = pl.ds(self.cols, self.width)
            grad = acc[...] / replicas
            moment = momentum_coef * mom[c, :, here] + grad
            mom_next[c, :, here] = moment
            base = snap[c, :, pl.ds(start, self.width)].astype(jnp.float32)
            self.res[c, p1, p2] = (base - outer_rate * (grad + momentum_coef * moment)).astype(jnp.bfloat16)
        when(p2 < self.n2 - 1)(lambda: self.gsend2(c, p2, True))
        when(p2 > 0)(lambda: self.gsend2(c, p2, False))
        self.spread1(c, p2)

    def gather(self, s, c):
        g = s - self.top
        p1, n1, p2, n2 = self.p1, self.n1, self.p2, self.n2
        if 1 <= g < n2:
            @when(p2 >= g)
            def _():
                self.arrive(self.res.at[c, p1, p2 - g], self.g2.at[c, p2 - g])
                when(p2 < n2 - 1)(lambda: self.gsend2(c, p2 - g, True))
                self.spread1(c, p2 - g)

            @when(p2 + g < n2)
            def _():
                self.arrive(self.res.at[c, p1, p2 + g], self.g2.at[c, p2 + g])
                when(p2 > 0)(lambda: self.gsend2(c, p2 + g, False))
                self.spread1(c, p2 + g)

        for h in range(n2):
            k = g - h
            if not 1 <= k < n1:
                continue
            for side in ((-1, 1) if h else (1,)):
                q2 = p2 + side * h

                @when(q2 >= 0 if side < 0 else q2 < n2)
                def _():
                    @when(p1 >= k)
                    def _():
                        self.arrive(self.res.at[c, p1 - k, q2], self.g1.at[c, p1 - k, q2])
                        when(p1 < n1 - 1)(lambda: self.gsend1(c, p1 - k, q2, True))

                    @when(p1 + k < n1)
                    def _():
                        self.arrive(self.res.at[c, p1 + k, q2], self.g1.at[c, p1 + k, q2])
                        when(p1 > 0)(lambda: self.gsend1(c, p1 + k, q2, False))


def exchange_kernel(dims, frag, inner, snapshot, momentum, bits, inner_v, res_a, res_b, mom_next, *scratch):
    outer, inner_n, chunks, share, wide = dims
    replicas = outer * inner_n
    frags = inner_v.shape[0]
    bbuf, snap, mom, acc_a, acc_b, wsem, bsem, ssem, msem = scratch[:9]
    bufs_a, bufs_b = (*scratch[9:14], res_a), (*scratch[14:19], res_b)
    sems_a, sems_b = scratch[19:31], scratch[31:43]
    me = lax.axis_index("replica")
    y, z = lax.rem(me, inner_n), lax.div(me, inner_n)
    line_y, line_z = (y, inner_n, 1), (z, outer, inner_n)

    def parts_at(r, draining):
        at_y, at_z = (r % inner_n, inner_n, 1), (r // inner_n, outer, inner_n)
        return (
            Part(bufs_a, sems_a, at_y, at_z, r, 0, wide, draining),
            Part(bufs_b, sems_b, at_z, at_y, r, wide, share - wide, draining),
        )

    def loads(c, slot):
        return (
            pltpu.make_async_copy(inner.at[0, :, c], inner_v.at[:, c], wsem.at[c]),
            pltpu.make_async_copy(bits.at[c], bbuf.at[slot], bsem.at[slot]),
            pltpu.make_async_copy(snapshot.at[c], snap.at[c], ssem.at[c]),
        )

    for copy in loads(0, 0):
        copy.start()
    mom_copy = pltpu.make_async_copy(momentum, mom, msem)
    mom_copy.start()

    barrier = pltpu.get_barrier_semaphore()
    count = 0
    for pos, n, step in (line_y, line_z):
        for delta, there in ((-step, pos > 0), (step, pos < n - 1)):
            @pl.when(there)
            def _():
                pl.semaphore_signal(barrier, inc=1, device_id={"replica": me + delta}, device_id_type=MESH)

            count = count + there.astype(jnp.int32)
    pl.semaphore_wait(barrier, count)
    mom_copy.wait()

    def round_chunk(c):
        slot = lax.rem(c, 2)

        @pl.when(c + 1 < chunks)
        def _():
            for copy in loads(c + 1, 1 - slot):
                copy.start()

        for copy in loads(c, slot):
            copy.wait()
        which = frag[0]
        for b in range(replicas):
            cols = slice(b * share, (b + 1) * share)
            chosen = inner_v[0, c, :, cols].astype(jnp.float32)
            for f in range(1, frags):
                chosen = jnp.where(which == f, inner_v[f, c, :, cols].astype(jnp.float32), chosen)
            scaled = grid_scale * (snap[c, :, cols].astype(jnp.float32) - chosen)
            lower = jnp.floor(scaled)
            raised = jnp.where(bbuf[slot, :, cols].astype(jnp.float32) < bit_levels * (scaled - lower), 1.0, 0.0)
            rounded = ((lower + raised) / grid_scale).astype(jnp.bfloat16)
            bz, by = b // inner_n, b % inner_n
            bufs_a[0][c, by, bz] = rounded[:, :wide]
            bufs_b[0][c, bz, by] = rounded[:, wide:]

    def stage(s, c, parts):
        for part in parts:
            part.hop1(s, c)
            part.hop2(s, c)
        if s == top:
            parts[0].update(c, snap, mom, mom_next, acc_a, replicas, share)
            parts[1].update(c, snap, mom, mom_next, acc_b, replicas, share)
        for part in parts:
            part.gather(s, c)

    top = inner_n + outer - 2
    stages = 2 * top + 1

    def at_my_place(todo, draining):
        for r in range(replicas):
            pl.when(me == r)(functools.partial(todo, parts_at(r, draining)))

    def tick(t, carry):
        def older(parts):
            for s in (range(stages - 1, 0, -1) if OLDEST_FIRST else range(1, stages)):
                c = t - s

                @pl.when(jnp.logical_and(c >= 0, c < chunks))
                def _():
                    stage(s, c, parts)

        if OLDEST_FIRST:
            at_my_place(older, False)

        @pl.when(t < chunks)
        def _():
            round_chunk(t)
            at_my_place(lambda parts: stage(0, t, parts), False)

        if not OLDEST_FIRST:
            at_my_place(older, False)
        return carry

    lax.fori_loop(0, chunks + stages - 1, tick, 0)

    def drain_at(parts):
        def drain(c, carry):
            for s in range(stages):
                stage(s, c, parts)
            return carry

        lax.fori_loop(0, chunks, drain, 0)

    at_my_place(drain_at, True)


def finish_kernel(frag, inner_v, res_a, res_b, mom_next, snap_out, mom_out, inner_out, snap_v, blend_v, mom_sem, pass_sem, snap_sem, blend_sem):
    frags, chunks = inner_v.shape[:2]
    n_y, n_z = res_a.shape[1], res_a.shape[2]
    wide = res_a.shape[4]
    share = wide + res_b.shape[4]
    which = frag[0]
    waits = [pltpu.make_async_copy(mom_next, mom_out, mom_sem)]
    for j in range(1, frags):
        other = lax.rem(which + j, frags)
        waits.append(pltpu.make_async_copy(inner_v.at[other], inner_out.at[0, other], pass_sem.at[j]))

    def puts(c):
        return (
            pltpu.make_async_copy(snap_v.at[c], snap_out.at[c], snap_sem.at[c]),
            pltpu.make_async_copy(blend_v.at[c], inner_out.at[0, which, c], blend_sem.at[c]),
        )

    for copy in waits:
        copy.start()

    def blend(c, carry):
        for bz in range(n_z):
            for by in range(n_y):
                first = (bz * n_y + by) * share
                for col, part in ((first, res_a[c, by, bz]), (first + wide, res_b[c, bz, by])):
                    cols = slice(col, col + part.shape[1])
                    snap_v[c, :, cols] = part
                    blend_v[c, :, cols] = (
                        blend_keep * inner_v[which, c, :, cols].astype(jnp.float32)
                        + (1.0 - blend_keep) * part.astype(jnp.float32)
                    ).astype(jnp.bfloat16)
        for copy in puts(c):
            copy.start()
        return carry

    lax.fori_loop(0, chunks, blend, 0)
    for copy in waits:
        copy.wait()

    def settle(c, carry):
        for copy in puts(c):
            copy.wait()
        return carry

    lax.fori_loop(0, chunks, settle, 0)


def body(inner_weights, snapshot, momentum, rand_bits, fragment):
    n = lax.axis_size("replica")
    outer, inner_n = grid_of(n)
    frags, rows, width = inner_weights.shape[1:]
    share = momentum.shape[1]
    wide = max(1, min(share // 128 - 1, round(0.6 * share / 128))) * 128
    narrow = share - wide
    chunks = rows // CHUNK_ROWS
    bf, f32 = jnp.bfloat16, jnp.float32
    dma = pltpu.SemaphoreType.DMA

    def bufs(n1, n2, w):
        full = (chunks, n1, n2, CHUNK_ROWS, w)
        line = (chunks, n2, CHUNK_ROWS, w)
        return [pltpu.VMEM(s, bf) for s in (full, full, full, line, line)]

    def sems(n1, n2):
        one, two, both = (chunks, n1), (chunks, n2), (chunks, n1, n2)
        return [dma(s) for s in (one,) * 3 + (two,) * 6 + (both,) * 3]

    scratch = [
        pltpu.VMEM((2, CHUNK_ROWS, width), jnp.int32),
        pltpu.VMEM((chunks, CHUNK_ROWS, width), bf),
        pltpu.VMEM((chunks, CHUNK_ROWS, share), f32),
        pltpu.VMEM((CHUNK_ROWS, wide), f32),
        pltpu.VMEM((CHUNK_ROWS, narrow), f32),
        dma((chunks,)), dma((2,)), dma((chunks,)), dma,
        *bufs(inner_n, outer, wide), *bufs(outer, inner_n, narrow),
        *sems(inner_n, outer), *sems(outer, inner_n),
    ]
    anywhere = pl.BlockSpec(memory_space=pl.ANY)
    in_vmem = pl.BlockSpec(memory_space=pltpu.VMEM)
    in_smem = pl.BlockSpec(memory_space=pltpu.SMEM)
    held = pl.pallas_call(
        functools.partial(exchange_kernel, (outer, inner_n, chunks, share, wide)),
        out_shape=(
            pltpu.VMEM((frags, chunks, CHUNK_ROWS, width), bf),
            pltpu.VMEM((chunks, inner_n, outer, CHUNK_ROWS, wide), bf),
            pltpu.VMEM((chunks, outer, inner_n, CHUNK_ROWS, narrow), bf),
            pltpu.VMEM((chunks, CHUNK_ROWS, share), f32),
        ),
        in_specs=[in_smem] + [pl.BlockSpec(memory_space=pltpu.HBM)] * 4,
        out_specs=(in_vmem,) * 4,
        scratch_shapes=scratch,
        compiler_params=pltpu.CompilerParams(
            collective_id=0, has_side_effects=True, vmem_limit_bytes=EXCHANGE_VMEM
        ),
        name="exchange",
    )(
        fragment,
        inner_weights.reshape(1, frags, chunks, CHUNK_ROWS, width),
        snapshot.reshape(chunks, CHUNK_ROWS, width),
        momentum.reshape(chunks, CHUNK_ROWS, share),
        rand_bits.reshape(chunks, CHUNK_ROWS, width),
    )

    new_snapshot, new_momentum, new_inner = pl.pallas_call(
        finish_kernel,
        in_specs=[in_smem] + [in_vmem] * 4,
        out_specs=(anywhere,) * 3,
        out_shape=(
            jax.ShapeDtypeStruct((chunks, CHUNK_ROWS, width), bf),
            jax.ShapeDtypeStruct((chunks, CHUNK_ROWS, share), f32),
            jax.ShapeDtypeStruct((1, frags, chunks, CHUNK_ROWS, width), bf),
        ),
        scratch_shapes=[
            pltpu.VMEM((chunks, CHUNK_ROWS, width), bf),
            pltpu.VMEM((chunks, CHUNK_ROWS, width), bf),
            dma, dma((frags,)), dma((chunks,)), dma((chunks,)),
        ],
        compiler_params=pltpu.CompilerParams(vmem_limit_bytes=FINISH_VMEM),
        name="finish",
    )(fragment, *held)
    return new_snapshot.reshape(rows, width), new_momentum.reshape(rows, share), new_inner.reshape(inner_weights.shape)


def solution(mesh):
    placed = (
        P("replica", None, "fsdp", None),
        P("fsdp", None),
        P("fsdp", "replica"),
        P("replica", "fsdp", None),
        P(),
    )
    return jax.shard_map(
        body,
        mesh=mesh,
        in_specs=placed,
        out_specs=(P("fsdp", None), P("fsdp", "replica"), P("replica", None, "fsdp", None)),
        check_vma=False,
    )
```

profile of v0, /device:TPU:0, one launch (start us, length us, event | category | flops | bytes accessed | tf_op | source)
XLA Modules:
  0.0 109.4 jit_solution(14180686015250665036)
XLA Ops:
  1.3 100.6 %exchange.1 = (bf16[4,8,32,8192]{3,2,1,0:T(8,128)(2,1)S(1)}, bf16[8,2,4,32,640]{4,3,2,1,0:T(8,128)(2,1)S(1)}, bf16[8,4,2,32,384]{4,3,2,1,0:T(8,128)(2,1)S(1)}, f32[8,32,1024]{2,1,0:T(8,128)S(1)}) custom-call(s32[1]{0:T(128)S(6)} %copy.8.frag, bf16[1,4,8,32,8192]{4,3,2,1,0:T(8,128)(2,1)} %bitcast.7, bf16[8,32,8192]{2,1,0:T(8,128)(2,1)} %bitcast.9, ...), custom_call_target="tpu_custom_call" | custom-call | tf_op jit(solution)/shard_map/exchange/pallas_call | solution.py:388
  101.8 7.6 %finish.1 = (bf16[8,32,8192]{2,1,0:T(8,128)(2,1)}, f32[8,32,1024]{2,1,0:T(8,128)}, bf16[1,4,8,32,8192]{4,3,2,1,0:T(8,128)(2,1)}) custom-call(s32[1]{0:T(128)S(6)} %copy.8.frag, bf16[4,8,32,8192]{3,2,1,0:T(8,128)(2,1)S(1)} %get-tuple-element.10.inner_v, bf16[8,2,4,32,640]{4,3,2,1,0:T(8,128)(2,1)S(1)} %get-tuple-element.11.res_a, ...), custom_call_target="tpu_custom_call" | custom-call | tf_op jit(solution)/shard_map/finish/pallas_call | solution.py:411
where the time goes:
time: 110 us; the launch traced here: 109 us
  Pallas kernels  108 us (98%)
  between operations  1.29 us (1%)
    pallas_call x1, Pallas kernels, body(): pl.pallas_call(functools.partial(exchange_kernel, (outer, inner_n, chunks...  101 us
    pallas_call x1, Pallas kernels, body(): pl.pallas_call(finish_kernel, in_specs=[in_smem] + [in_vmem] * 4, out_spe...  7.57 us

commit v1 on v0

--- a/solution.py
+++ b/solution.py
@@ -14,7 +14,7 @@
 bit_levels = 4096.0
 MESH = pl.DeviceIdType.MESH
 CHUNK_ROWS = 32
-OLDEST_FIRST = True
+TUNED = [(2, 1, 2), (8, 0, 14), (7, 0, 9), (-1, 0, 0), (4, 1, 3), (4, 0, 4), (0, 1, 0), (5, 0, 5), (7, 1, 12), (8, 1, 23), (3, 1, 2), (6, 0, 6), (0, 0, 0), (1, 1, 1), (3, 0, 3), (6, 1, 4), (5, 1, 3), (1, 0, 1), (2, 0, 2)]
 EXCHANGE_VMEM = 42 << 20
 FINISH_VMEM = 10 << 20
 
@@ -28,6 +28,13 @@
 def grid_of(n):
     inner = max(k for k in range(1, n + 1) if n % k == 0 and k * k <= n)
     return n // inner, inner
+
+
+def order_of(stages):
+    if stages == max(s for s, _, _ in TUNED) + 1:
+        return TUNED
+    older = [(s, part, s) for s in range(stages - 1, 0, -1) for part in (0, 1)]
+    return [*older, (-1, 0, 0), (0, 0, 0), (0, 1, 0)]
 
 
 class Part:
@@ -254,15 +261,12 @@
             bufs_a[0][c, by, bz] = rounded[:, :wide]
             bufs_b[0][c, bz, by] = rounded[:, wide:]
 
-    def stage(s, c, parts):
-        for part in parts:
-            part.hop1(s, c)
-            part.hop2(s, c)
+    def stage(s, c, part):
+        part.hop1(s, c)
+        part.hop2(s, c)
         if s == top:
-            parts[0].update(c, snap, mom, mom_next, acc_a, replicas, share)
-            parts[1].update(c, snap, mom, mom_next, acc_b, replicas, share)
-        for part in parts:
-            part.gather(s, c)
+            part.update(c, snap, mom, mom_next, acc_b if part.cols else acc_a, replicas, share)
+        part.gather(s, c)
 
     top = inner_n + outer - 2
     stages = 2 * top + 1
@@ -271,33 +275,30 @@
         for r in range(replicas):
             pl.when(me == r)(functools.partial(todo, parts_at(r, draining)))
 
+    plan = order_of(stages)
+    split = plan.index((-1, 0, 0))
+
     def tick(t, carry):
-        def older(parts):
-            for s in (range(stages - 1, 0, -1) if OLDEST_FIRST else range(1, stages)):
-                c = t - s
+        def run(entries, parts):
+            for s, which_part, lag in entries:
+                c = t - lag
 
                 @pl.when(jnp.logical_and(c >= 0, c < chunks))
                 def _():
-                    stage(s, c, parts)
-
-        if OLDEST_FIRST:
-            at_my_place(older, False)
-
-        @pl.when(t < chunks)
-        def _():
-            round_chunk(t)
-            at_my_place(lambda parts: stage(0, t, parts), False)
-
-        if not OLDEST_FIRST:
-            at_my_place(older, False)
+                    stage(s, c, parts[which_part])
+
+        at_my_place(functools.partial(run, plan[:split]), False)
+        pl.when(t < chunks)(functools.partial(round_chunk, t))
+        at_my_place(functools.partial(run, plan[split + 1:]), False)
         return carry
 
-    lax.fori_loop(0, chunks + stages - 1, tick, 0)
+    lax.fori_loop(0, chunks + max(lag for _, _, lag in plan), tick, 0)
 
     def drain_at(parts):
         def drain(c, carry):
             for s in range(stages):
-                stage(s, c, parts)
+                for part in parts:
+                    stage(s, c, part)
             return carry
 
         lax.fori_loop(0, chunks, drain, 0)

time: 110 us -> 106 us (0.964)
  Pallas kernels: 108 us -> 104 us
    pallas_call x1, Pallas kernels: 101 us -> 96.5 us  [body(): pl.pallas_call(functools.partial(exchange_kernel, (outer, inner_n, chunks...]
where the time goes in v1:
time: 106 us; the launch traced here: 105 us
  Pallas kernels  104 us (98%)
  between operations  1.29 us (1%)
    pallas_call x1, Pallas kernels, body(): pl.pallas_call(functools.partial(exchange_kernel, (outer, inner_n, chunks...  96.5 us
    pallas_call x1, Pallas kernels, body(): pl.pallas_call(finish_kernel, in_specs=[in_smem] + [in_vmem] * 4, out_spe...  7.57 us

profile of v1, /device:TPU:0, one launch (start us, length us, event | category | flops | bytes accessed | tf_op | source)
XLA Modules:
  0.0 105.3 jit_solution(12682667040762417548)
XLA Ops:
  1.3 96.5 %exchange.1 = (bf16[4,8,32,8192]{3,2,1,0:T(8,128)(2,1)S(1)}, bf16[8,2,4,32,640]{4,3,2,1,0:T(8,128)(2,1)S(1)}, bf16[8,4,2,32,384]{4,3,2,1,0:T(8,128)(2,1)S(1)}, f32[8,32,1024]{2,1,0:T(8,128)S(1)}) custom-call(s32[1]{0:T(128)S(6)} %copy.8.frag, bf16[1,4,8,32,8192]{4,3,2,1,0:T(8,128)(2,1)} %bitcast.7, bf16[8,32,8192]{2,1,0:T(8,128)(2,1)} %bitcast.9, ...), custom_call_target="tpu_custom_call" | custom-call | tf_op jit(solution)/shard_map/exchange/pallas_call | solution.py:389
  97.8 7.6 %finish.1 = (bf16[8,32,8192]{2,1,0:T(8,128)(2,1)}, f32[8,32,1024]{2,1,0:T(8,128)}, bf16[1,4,8,32,8192]{4,3,2,1,0:T(8,128)(2,1)}) custom-call(s32[1]{0:T(128)S(6)} %copy.8.frag, bf16[4,8,32,8192]{3,2,1,0:T(8,128)(2,1)S(1)} %get-tuple-element.10.inner_v, bf16[8,2,4,32,640]{4,3,2,1,0:T(8,128)(2,1)S(1)} %get-tuple-element.11.res_a, ...), custom_call_target="tpu_custom_call" | custom-call | tf_op jit(solution)/shard_map/finish/pallas_call | solution.py:412

commit v2 on v0

v2 whole, which is shorter than its diff:
```python
import functools
import itertools

import jax
import jax.numpy as jnp
from jax import lax
from jax.experimental import pallas as pl
from jax.experimental.pallas import tpu as pltpu
from jax.sharding import PartitionSpec as P

momentum_coef = 0.9
outer_rate = 0.7
blend_keep = 0.5
grid_scale = 4.0
bit_levels = 4096.0
MESH = pl.DeviceIdType.MESH
CHUNK_ROWS = 32
TUNED = [
    (0, 3, 0, 12), (0, 0, 0, 3), (0, 4, 1, 11), (0, 2, 1, 6), (1, 6, 0, 62),
    (0, 5, 1, 20), (1, 4, 1, 11), (0, 1, 1, 4), (0, 6, 0, 24), (1, 4, 0, 11),
    (0, 2, 0, 10), (0, 8, 0, 78), (1, 3, 1, 9), (0, 4, 0, 16), (1, 3, 0, 10),
    (0, 7, 1, 33), (0, 7, 0, 26), (-1, -1, 0, 0), (1, 2, 1, 7), (1, 5, 0, 14),
    (0, 1, 0, 7), (1, 1, 1, 6), (1, 0, 1, 2), (0, 8, 1, 79), (1, 1, 0, 4),
    (1, 6, 1, 67), (0, 5, 0, 21), (1, 5, 1, 12), (0, 6, 1, 26), (1, 2, 0, 8),
    (0, 3, 1, 9), (1, 0, 0, 1), (0, 0, 1, 0),
]
EXCHANGE_VMEM = 42 << 20
FINISH_VMEM = 10 << 20


def grid_of(n):
    inner = max(k for k in range(1, n + 1) if n % k == 0 and k * k <= n)
    return n // inner, inner


def owners(n):
    ends = n // 4
    return ([*range(ends), *range(n - (n // 2 - ends), n)], [*range(ends, ends + n // 2)])


def depth(n, group):
    return max(max(q, n - 1 - q) for q in group)


def stages_of(n_y, n_z, kind):
    return 2 * (n_y - 1) + 2 * depth(n_z, owners(n_z)[kind]) + 1


def order_of(n_y, n_z):
    counts = [stages_of(n_y, n_z, kind) for kind in (0, 1)]
    if counts == [max(s for k, s, _, _ in TUNED if k == kind) + 1 for kind in (0, 1)]:
        return TUNED
    order = []
    for s in range(max(counts) - 1, 0, -1):
        order += [(kind, s, part, s) for kind in (0, 1) if s < counts[kind] for part in (0, 1)]
    return [*order, (-1, -1, 0, 0), *((kind, 0, part, 0) for kind in (0, 1) for part in (0, 1))]


class Line:
    def __init__(self, pos, n, step, me):
        self.pos, self.n, self.step, self.me = pos, n, step, me

    def send(self, src, dst, send_sem, recv_sem, right):
        copy = pltpu.make_async_remote_copy(
            src_ref=src, dst_ref=dst, send_sem=send_sem, recv_sem=recv_sem,
            device_id={"replica": self.me + (self.step if right else -self.step)}, device_id_type=MESH,
        )
        copy.start()

    def settle(self, ref, sem):
        return pltpu.make_async_remote_copy(
            src_ref=ref, dst_ref=ref, send_sem=sem, recv_sem=sem,
            device_id={"replica": self.me}, device_id_type=MESH,
        )

    def arrive(self, dst, recv_sem):
        self.settle(dst, recv_sem).wait_recv()

    def reduce(self, h, group, i, block, arrived, from_left, from_right, sems, add):
        send_sem, left_sem, right_sem = sems
        p, n = self.pos, self.n
        for slot, q in sorted(enumerate(group), key=lambda e: -e[1]):
            if p == h and p <= q and (h > 0 or q > 0):
                if p > 0:
                    self.arrive(from_left.at[i, slot], left_sem.at[i, slot])
                    if p < q or arrived:
                        add(block(slot), from_left.at[i, slot])
                if p < q:
                    self.send(block(slot), from_left.at[i, slot], send_sem, left_sem.at[i, slot], True)
        for slot, q in enumerate(group):
            if p == n - 1 - h and p >= q and (h > 0 or q < n - 1):
                if p < n - 1:
                    self.arrive(from_right.at[i, slot], right_sem.at[i, slot])
                    if p > q or arrived:
                        add(block(slot), from_right.at[i, slot])
                if p > q:
                    self.send(block(slot), from_right.at[i, slot], send_sem, right_sem.at[i, slot], False)

    def spread(self, k, group, i, block, sems):
        recv_sem, right_sem, left_sem = sems
        p, n = self.pos, self.n
        for slot, q in enumerate(group):
            here = block(slot)
            if k == 0 and p != q or k > 0 and abs(p - q) != k:
                continue
            if k > 0:
                self.arrive(here, recv_sem.at[i, slot])
            if p < n - 1 and p >= q:
                self.send(here, here, right_sem, recv_sem.at[i, slot], True)
            if p > 0 and p <= q:
                self.send(here, here, left_sem, recv_sem.at[i, slot], False)


class Part:
    def __init__(self, refs, sems, line_y, line_z, ctx, y_first):
        self.own, self.yr, self.yl, self.zr, self.zl, self.res = refs
        self.sy, self.sz, self.gy, self.gz = (sems[j : j + 3] for j in (0, 3, 6, 9))
        self.line_y, self.line_z, self.y_first = line_y, line_z, y_first
        self.ctx = ctx

    def add(self, block, recv):
        block[...] = block[...] + recv[...]

    def update(self, i, rc, slot):
        snap, mom, mom_next, acc, replicas, share, cols, width = self.ctx
        y, z = self.line_y.pos, self.line_z.pos
        line, block = (self.line_z, slot) if self.y_first else (self.line_y, y)
        left, right = (self.zr, self.zl) if self.y_first else (self.yr, self.yl)
        here = (i, y, slot) if self.y_first else (i, slot, y)
        acc[...] = self.own[here].astype(jnp.float32)
        if line.pos > 0:
            acc[...] += left[i, block].astype(jnp.float32)
        if line.pos < line.n - 1:
            acc[...] += right[i, block].astype(jnp.float32)
        start = (z * self.line_y.n + y) * share + cols
        strip = pl.ds(cols, width)
        grad = acc[...] / replicas
        moment = momentum_coef * mom[rc, :, strip] + grad
        mom_next[rc, :, strip] = moment
        base = snap[rc, :, pl.ds(start, width)].astype(jnp.float32)
        self.res[here] = (base - outer_rate * (grad + momentum_coef * moment)).astype(jnp.bfloat16)

    def stage(self, s, i, rc, kind):
        line_y, line_z = self.line_y, self.line_z
        y, z, last_y = line_y.pos, line_z.pos, line_y.n - 1
        rows, group = [*range(line_y.n)], owners(line_z.n)[kind]
        sent, *landed = self.sz
        on_z = (sent.at[kind], *landed)
        sent, *landed = self.sy
        on_y = (sent.at[0], *landed)
        landed, right, left = self.gz
        out_z = (landed, right.at[kind], left.at[kind])
        landed, right, left = self.gy
        out_y = (landed, right.at[0], left.at[0])
        far = depth(line_z.n, group)
        slot = group.index(z) if z in group else None
        if self.y_first:
            if s <= last_y:
                line_y.reduce(s, rows, i, lambda q: self.own.at[i, q], True, self.yr, self.yl, on_y, self.add)
            h = s - last_y
            if 0 <= h <= far:
                line_z.reduce(h, group, i, lambda q: self.own.at[i, y, q], False, self.zr, self.zl, on_z, self.add)
            if h == far and slot is not None:
                self.update(i, rc, slot)
            if 0 <= h - far <= far:
                line_z.spread(h - far, group, i, lambda q: self.res.at[i, y, q], out_z)
            if 0 <= h - 2 * far <= last_y:
                line_y.spread(h - 2 * far, rows, i, lambda q: self.res.at[i, q], out_y)
        else:
            if s <= far:
                line_z.reduce(s, group, i, lambda q: self.own.at[i, q], True, self.zr, self.zl, on_z, self.add)
            h = s - far
            if slot is not None and 0 <= h <= last_y:
                line_y.reduce(h, rows, i, lambda q: self.own.at[i, slot, q], False, self.yr, self.yl, on_y, self.add)
            if slot is not None and h == last_y:
                self.update(i, rc, slot)
            if slot is not None and 0 <= h - last_y <= last_y:
                line_y.spread(h - last_y, rows, i, lambda q: self.res.at[i, slot, q], out_y)
            k = h - 2 * last_y
            if 0 <= k <= far:
                line_z.spread(k, group, i, lambda q: self.res.at[i, q], out_z)


    def settle(self, chunks):
        line_y, line_z = self.line_y, self.line_z
        y, z = line_y.pos, line_z.pos
        waits = []

        def on_y(ref, count, sem):
            waits.append((ref.at[:, :count] if self.y_first else ref.at[:chunks, 0, :count], sem.at[0], count))

        def on_z(ref, count, sem, kind):
            waits.append((ref.at[:chunks, 0, :count] if self.y_first else ref.at[:chunks, :count], sem.at[kind], count))

        on_y(self.own, line_y.n - 1, self.sy[0])
        on_y(self.res, (y + 1) * (y < line_y.n - 1), self.gy[1])
        on_y(self.res, (line_y.n - y) * (y > 0), self.gy[2])
        for kind, group in enumerate(owners(line_z.n)):
            on_z(self.own, sum(q != z for q in group), self.sz[0], kind)
            on_z(self.res, sum(q <= z for q in group) * (z < line_z.n - 1), self.gz[1], kind)
            on_z(self.res, sum(q >= z for q in group) * (z > 0), self.gz[2], kind)
        for ref, sem, count in waits:
            if count:
                line_y.settle(ref, sem).wait_send()


def exchange_kernel(dims, frag, inner, snapshot, momentum, bits, inner_v, res_a, res_b, mom_next, *scratch):
    n_z, n_y, chunks, share, wide = dims
    replicas, total = n_z * n_y, 2 * chunks
    frags = inner_v.shape[0]
    bbuf, snap, mom, acc_a, acc_b, wsem, bsem, ssem, msem = scratch[:9]
    refs_a, refs_b = (*scratch[9:14], res_a), (*scratch[14:19], res_b)
    sems_a, sems_b = scratch[19:31], scratch[31:43]
    me = lax.axis_index("replica")
    y, z = lax.rem(me, n_y), lax.div(me, n_y)
    groups = owners(n_z)
    strip = n_y * share

    def parts_at(r):
        line_y = Line(r % n_y, n_y, 1, r)
        line_z = Line(r // n_y, n_z, n_y, r)
        ctx = (snap, mom, mom_next)
        return (
            Part(refs_a, sems_a, line_y, line_z, (*ctx, acc_a, replicas, share, 0, wide), True),
            Part(refs_b, sems_b, line_y, line_z, (*ctx, acc_b, replicas, share, wide, share - wide), False),
        )

    def loads(rc, kind):
        i = 2 * rc + kind
        copies = []
        for slot, owner in enumerate(groups[kind]):
            cols = slice(owner * strip, (owner + 1) * strip)
            copies += [
                pltpu.make_async_copy(inner.at[0, :, rc, :, cols], inner_v.at[:, rc, :, cols], wsem.at[i, slot]),
                pltpu.make_async_copy(bits.at[rc, :, cols], bbuf.at[kind, slot], bsem.at[kind, slot]),
                pltpu.make_async_copy(snapshot.at[rc, :, cols], snap.at[rc, :, cols], ssem.at[i, slot]),
            ]
        return copies

    for copy in loads(0, 0):
        copy.start()
    mom_copy = pltpu.make_async_copy(momentum, mom, msem)
    mom_copy.start()

    barrier = pltpu.get_barrier_semaphore()
    count = 0
    for pos, n, step in ((y, n_y, 1), (z, n_z, n_y)):
        for delta, there in ((-step, pos > 0), (step, pos < n - 1)):
            @pl.when(there)
            def _():
                pl.semaphore_signal(barrier, inc=1, device_id={"replica": me + delta}, device_id_type=MESH)

            count = count + there.astype(jnp.int32)

    def round_chunk(rc, kind):
        @pl.when(rc + kind < chunks)
        def _():
            for copy in loads(rc + kind, 1 - kind):
                copy.start()

        for copy in loads(rc, kind):
            copy.wait()
        which = frag[0]
        i = 2 * rc + kind
        for slot, owner in enumerate(groups[kind]):
            for by in range(n_y):
                cols = slice(owner * strip + by * share, owner * strip + (by + 1) * share)
                chosen = inner_v[0, rc, :, cols]
                for f in range(1, frags):
                    chosen = jnp.where(which == f, inner_v[f, rc, :, cols], chosen)
                scaled = grid_scale * (snap[rc, :, cols].astype(jnp.float32) - chosen.astype(jnp.float32))
                lower = jnp.floor(scaled)
                drawn = bbuf[kind, slot, :, by * share : (by + 1) * share].astype(jnp.float32)
                raised = jnp.where(drawn < bit_levels * (scaled - lower), 1.0, 0.0)
                rounded = ((lower + raised) / grid_scale).astype(jnp.bfloat16)
                refs_a[0][i, by, slot] = rounded[:, :wide]
                refs_b[0][i, slot, by] = rounded[:, wide:]

    plan = order_of(n_y, n_z)
    split = [kind for kind, _, _, _ in plan].index(-1)
    last = max(lag for _, _, _, lag in plan)

    def at_my_place(todo):
        for r in range(replicas):
            pl.when(me == r)(functools.partial(todo, parts_at(r)))

    def entries_of(parity, entries):
        for kind, s, part, lag in entries:
            if (parity - lag - kind) % 2 == 0:
                yield (parity - lag - kind) // 2, kind, s, part

    def two_ticks(u, carry):
        def run(entries, parts):
            for ahead, some in itertools.groupby(entries, key=lambda e: e[0]):
                rc = u + ahead

                @pl.when(jnp.logical_and(rc >= 0, rc < chunks))
                def _():
                    for _, kind, s, part in some:
                        parts[part].stage(s, 2 * rc + kind, rc, kind)

        before, after = ([[*entries_of(parity, p)] for parity in (0, 1)] for p in (plan[:split], plan[split + 1 :]))
        at_my_place(functools.partial(run, before[0]))
        pl.when(u < chunks)(functools.partial(round_chunk, u, 1))
        at_my_place(functools.partial(run, after[0] + before[1]))
        pl.when(u + 1 < chunks)(functools.partial(round_chunk, u + 1, 0))
        at_my_place(functools.partial(run, after[1]))
        return carry

    round_chunk(0, 0)
    pl.semaphore_wait(barrier, count)
    mom_copy.wait()
    lax.fori_loop(0, pl.cdiv(total + last, 2), two_ticks, 0)

    def settle(parts):
        for part in parts:
            part.settle(chunks)

    at_my_place(settle)


def finish_kernel(frag, inner_v, res_a, res_b, mom_next, snap_out, mom_out, inner_out, snap_v, blend_v, mom_sem, pass_sem, snap_sem, blend_sem):
    frags, chunks = inner_v.shape[:2]
    n_y, n_z = res_a.shape[1], 2 * res_a.shape[2]
    wide = res_a.shape[4]
    share = wide + res_b.shape[4]
    which = frag[0]
    waits = [pltpu.make_async_copy(mom_next, mom_out, mom_sem)]
    for j in range(1, frags):
        other = lax.rem(which + j, frags)
        waits.append(pltpu.make_async_copy(inner_v.at[other], inner_out.at[0, other], pass_sem.at[j]))

    def puts(c):
        return (
            pltpu.make_async_copy(snap_v.at[c], snap_out.at[c], snap_sem.at[c]),
            pltpu.make_async_copy(blend_v.at[c], inner_out.at[0, which, c], blend_sem.at[c]),
        )

    for copy in waits:
        copy.start()

    def blend(c, carry):
        for kind, group in enumerate(owners(n_z)):
            i = 2 * c + kind
            for slot, by in ((slot, by) for slot in range(len(group)) for by in range(n_y)):
                first = (group[slot] * n_y + by) * share
                for col, part in ((first, res_a[i, by, slot]), (first + wide, res_b[i, slot, by])):
                    cols = slice(col, col + part.shape[1])
                    snap_v[c, :, cols] = part
                    blend_v[c, :, cols] = (
                        blend_keep * inner_v[which, c, :, cols].astype(jnp.float32)
                        + (1.0 - blend_keep) * part.astype(jnp.float32)
                    ).astype(jnp.bfloat16)
        for copy in puts(c):
            copy.start()
        return carry

    lax.fori_loop(0, chunks, blend, 0)
    for copy in waits:
        copy.wait()

    def settle(c, carry):
        for copy in puts(c):
            copy.wait()
        return carry

    lax.fori_loop(0, chunks, settle, 0)


def body(inner_weights, snapshot, momentum, rand_bits, fragment):
    n = lax.axis_size("replica")
    outer, inner_n = grid_of(n)
    frags, rows, width = inner_weights.shape[1:]
    share = momentum.shape[1]
    wide = max(1, min(share // 128 - 1, round(0.6 * share / 128))) * 128
    narrow = share - wide
    chunks = rows // CHUNK_ROWS
    bf, f32 = jnp.bfloat16, jnp.float32
    dma = pltpu.SemaphoreType.DMA

    half, total = outer // 2, 2 * chunks

    def bufs(w, y_first):
        block = (CHUNK_ROWS, w)
        own = (total, inner_n, half, *block) if y_first else (total, half, inner_n, *block)
        line_y = own if y_first else (total, inner_n, *block)
        line_z = (total, half, *block) if y_first else own
        return [pltpu.VMEM(s, bf) for s in (own, line_y, line_y, line_z, line_z)]

    def sems():
        on_y, on_z = (total, inner_n), (total, half)
        one, two = (1,), (2,)
        return [dma(s) for s in (one, on_y, on_y, two, on_z, on_z, on_y, one, one, on_z, two, two)]

    scratch = [
        pltpu.VMEM((2, half, CHUNK_ROWS, inner_n * share), jnp.int32),
        pltpu.VMEM((chunks, CHUNK_ROWS, width), bf),
        pltpu.VMEM((chunks, CHUNK_ROWS, share), f32),
        pltpu.VMEM((CHUNK_ROWS, wide), f32),
        pltpu.VMEM((CHUNK_ROWS, narrow), f32),
        dma((total, half)), dma((2, half)), dma((total, half)), dma,
        *bufs(wide, True), *bufs(narrow, False),
        *sems(), *sems(),
    ]
    anywhere = pl.BlockSpec(memory_space=pl.ANY)
    in_vmem = pl.BlockSpec(memory_space=pltpu.VMEM)
    in_smem = pl.BlockSpec(memory_space=pltpu.SMEM)
    held = pl.pallas_call(
        functools.partial(exchange_kernel, (outer, inner_n, chunks, share, wide)),
        out_shape=(
            pltpu.VMEM((frags, chunks, CHUNK_ROWS, width), bf),
            pltpu.VMEM((total, inner_n, half, CHUNK_ROWS, wide), bf),
            pltpu.VMEM((total, half, inner_n, CHUNK_ROWS, narrow), bf),
            pltpu.VMEM((chunks, CHUNK_ROWS, share), f32),
        ),
        in_specs=[in_smem] + [pl.BlockSpec(memory_space=pltpu.HBM)] * 4,
        out_specs=(in_vmem,) * 4,
        scratch_shapes=scratch,
        compiler_params=pltpu.CompilerParams(
            collective_id=0, has_side_effects=True, vmem_limit_bytes=EXCHANGE_VMEM
        ),
        name="exchange",
    )(
        fragment,
        inner_weights.reshape(1, frags, chunks, CHUNK_ROWS, width),
        snapshot.reshape(chunks, CHUNK_ROWS, width),
        momentum.reshape(chunks, CHUNK_ROWS, share),
        rand_bits.reshape(chunks, CHUNK_ROWS, width),
    )

    new_snapshot, new_momentum, new_inner = pl.pallas_call(
        finish_kernel,
        in_specs=[in_smem] + [in_vmem] * 4,
        out_specs=(anywhere,) * 3,
        out_shape=(
            jax.ShapeDtypeStruct((chunks, CHUNK_ROWS, width), bf),
            jax.ShapeDtypeStruct((chunks, CHUNK_ROWS, share), f32),
            jax.ShapeDtypeStruct((1, frags, chunks, CHUNK_ROWS, width), bf),
        ),
        scratch_shapes=[
            pltpu.VMEM((chunks, CHUNK_ROWS, width), bf),
            pltpu.VMEM((chunks, CHUNK_ROWS, width), bf),
            dma, dma((frags,)), dma((chunks,)), dma((chunks,)),
        ],
        compiler_params=pltpu.CompilerParams(vmem_limit_bytes=FINISH_VMEM),
        name="finish",
    )(fragment, *held)
    return new_snapshot.reshape(rows, width), new_momentum.reshape(rows, share), new_inner.reshape(inner_weights.shape)


def solution(mesh):
    placed = (
        P("replica", None, "fsdp", None),
        P("fsdp", None),
        P("fsdp", "replica"),
        P("replica", "fsdp", None),
        P(),
    )
    return jax.shard_map(
        body,
        mesh=mesh,
        in_specs=placed,
        out_specs=(P("fsdp", None), P("fsdp", "replica"), P("replica", None, "fsdp", None)),
        check_vma=False,
    )
```

time: 110 us -> 97.7 us (0.89)
  Pallas kernels: 108 us -> 96.1 us
    pallas_call x1, Pallas kernels: 101 us -> 88.6 us  [body(): pl.pallas_call(functools.partial(exchange_kernel, (outer, inner_n, chunks...]
where the time goes in v2:
time: 97.7 us; the launch traced here: 97.4 us
  Pallas kernels  96.1 us (98%)
  between operations  1.29 us (1%)
    pallas_call x1, Pallas kernels, body(): pl.pallas_call(functools.partial(exchange_kernel, (outer, inner_n, chunks...  88.6 us
    pallas_call x1, Pallas kernels, body(): pl.pallas_call(finish_kernel, in_specs=[in_smem] + [in_vmem] * 4, out_spe...  7.57 us

profile of v2, /device:TPU:0, one launch (start us, length us, event | category | flops | bytes accessed | tf_op | source)
XLA Modules:
  0.0 97.4 jit_solution(4213534500706488930)
XLA Ops:
  1.3 88.6 %exchange.1 = (bf16[4,8,32,8192]{3,2,1,0:T(8,128)(2,1)S(1)}, bf16[16,2,2,32,640]{4,3,2,1,0:T(8,128)(2,1)S(1)}, bf16[16,2,2,32,384]{4,3,2,1,0:T(8,128)(2,1)S(1)}, f32[8,32,1024]{2,1,0:T(8,128)S(1)}) custom-call(s32[1]{0:T(128)S(6)} %copy.8.frag, bf16[1,4,8,32,8192]{4,3,2,1,0:T(8,128)(2,1)} %bitcast.7, bf16[8,32,8192]{2,1,0:T(8,128)(2,1)} %bitcast.9, ...), custom_call_target="tpu_custom_call" | custom-call | tf_op jit(solution)/shard_map/exchange/pallas_call | solution.py:408
  89.9 7.6 %finish.1 = (bf16[8,32,8192]{2,1,0:T(8,128)(2,1)}, f32[8,32,1024]{2,1,0:T(8,128)}, bf16[1,4,8,32,8192]{4,3,2,1,0:T(8,128)(2,1)}) custom-call(s32[1]{0:T(128)S(6)} %copy.8.frag, bf16[4,8,32,8192]{3,2,1,0:T(8,128)(2,1)S(1)} %get-tuple-element.10.inner_v, bf16[16,2,2,32,640]{4,3,2,1,0:T(8,128)(2,1)S(1)} %get-tuple-element.11.res_a, ...), custom_call_target="tpu_custom_call" | custom-call | tf_op jit(solution)/shard_map/finish/pallas_call | solution.py:431

commit v3 on v2

--- a/solution.py
+++ b/solution.py
@@ -16,13 +16,13 @@
 MESH = pl.DeviceIdType.MESH
 CHUNK_ROWS = 32
 TUNED = [
-    (0, 3, 0, 12), (0, 0, 0, 3), (0, 4, 1, 11), (0, 2, 1, 6), (1, 6, 0, 62),
-    (0, 5, 1, 20), (1, 4, 1, 11), (0, 1, 1, 4), (0, 6, 0, 24), (1, 4, 0, 11),
-    (0, 2, 0, 10), (0, 8, 0, 78), (1, 3, 1, 9), (0, 4, 0, 16), (1, 3, 0, 10),
-    (0, 7, 1, 33), (0, 7, 0, 26), (-1, -1, 0, 0), (1, 2, 1, 7), (1, 5, 0, 14),
-    (0, 1, 0, 7), (1, 1, 1, 6), (1, 0, 1, 2), (0, 8, 1, 79), (1, 1, 0, 4),
-    (1, 6, 1, 67), (0, 5, 0, 21), (1, 5, 1, 12), (0, 6, 1, 26), (1, 2, 0, 8),
-    (0, 3, 1, 9), (1, 0, 0, 1), (0, 0, 1, 0),
+    (0, 1, 0, 7), (0, 0, 1, 1), (1, 0, 0, 1), (0, 5, 1, 19), (0, 2, 1, 6),
+    (1, 6, 0, 22), (0, 2, 0, 10), (1, 6, 1, 32), (1, 4, 1, 10), (1, 0, 1, 2),
+    (0, 8, 0, 35), (1, 1, 1, 6), (0, 7, 1, 32), (1, 4, 0, 10), (-1, -1, 0, 0),
+    (0, 5, 0, 22), (1, 5, 1, 11), (0, 4, 0, 17), (0, 4, 1, 11), (0, 1, 1, 4),
+    (1, 3, 0, 8), (0, 6, 1, 27), (0, 7, 0, 28), (1, 3, 1, 8), (0, 3, 0, 11),
+    (0, 3, 1, 7), (1, 2, 1, 7), (0, 0, 0, 4), (1, 2, 0, 6), (0, 8, 1, 35),
+    (1, 1, 0, 3), (0, 6, 0, 25), (1, 5, 0, 11),
 ]
 EXCHANGE_VMEM = 42 << 20
 FINISH_VMEM = 10 << 20
@@ -279,6 +279,7 @@
     plan = order_of(n_y, n_z)
     split = [kind for kind, _, _, _ in plan].index(-1)
     last = max(lag for _, _, _, lag in plan)
+    first = min(lag for kind, s, _, lag in plan if kind >= 0 and s == n_y - 1 + depth(n_z, groups[kind]))
 
     def at_my_place(todo):
         for r in range(replicas):
@@ -289,8 +290,8 @@
             if (parity - lag - kind) % 2 == 0:
                 yield (parity - lag - kind) // 2, kind, s, part
 
-    def two_ticks(u, carry):
-        def run(entries, parts):
+    def two_ticks(u, carry, parts):
+        def run(entries):
             for ahead, some in itertools.groupby(entries, key=lambda e: e[0]):
                 rc = u + ahead
 
@@ -299,18 +300,23 @@
                     for _, kind, s, part in some:
                         parts[part].stage(s, 2 * rc + kind, rc, kind)
 
+        pl.when(u == first // 2)(mom_copy.wait)
         before, after = ([[*entries_of(parity, p)] for parity in (0, 1)] for p in (plan[:split], plan[split + 1 :]))
-        at_my_place(functools.partial(run, before[0]))
+        run(before[0])
         pl.when(u < chunks)(functools.partial(round_chunk, u, 1))
-        at_my_place(functools.partial(run, after[0] + before[1]))
+        run(after[0] + before[1])
         pl.when(u + 1 < chunks)(functools.partial(round_chunk, u + 1, 0))
-        at_my_place(functools.partial(run, after[1]))
+        run(after[1])
         return carry
 
     round_chunk(0, 0)
     pl.semaphore_wait(barrier, count)
-    mom_copy.wait()
-    lax.fori_loop(0, pl.cdiv(total + last, 2), two_ticks, 0)
+    ticks = pl.cdiv(total + last, 2)
+
+    def all_ticks(parts):
+        lax.fori_loop(0, ticks, lambda u, carry: two_ticks(u, carry, parts), 0)
+
+    at_my_place(all_ticks)
 
     def settle(parts):
         for part in parts:

time: 97.7 us -> 97.4 us (level)
  no operation moved by 1% of the time
where the time goes in v3:
time: 97.4 us; the launch traced here: 97.2 us
  Pallas kernels  95.9 us (98%)
  between operations  1.29 us (1%)
    pallas_call x1, Pallas kernels, body(): pl.pallas_call(functools.partial(exchange_kernel, (outer, inner_n, chunks...  88.3 us
    pallas_call x1, Pallas kernels, body(): pl.pallas_call(finish_kernel, in_specs=[in_smem] + [in_vmem] * 4, out_spe...  7.57 us

profile of v3, /device:TPU:0, one launch (start us, length us, event | category | flops | bytes accessed | tf_op | source)
XLA Modules:
  0.0 97.2 jit_solution(14595218947322789829)
XLA Ops:
  1.3 88.3 %exchange.1 = (bf16[4,8,32,8192]{3,2,1,0:T(8,128)(2,1)S(1)}, bf16[16,2,2,32,640]{4,3,2,1,0:T(8,128)(2,1)S(1)}, bf16[16,2,2,32,384]{4,3,2,1,0:T(8,128)(2,1)S(1)}, f32[8,32,1024]{2,1,0:T(8,128)S(1)}) custom-call(s32[1]{0:T(128)S(6)} %copy.8.frag, bf16[1,4,8,32,8192]{4,3,2,1,0:T(8,128)(2,1)} %bitcast.7, bf16[8,32,8192]{2,1,0:T(8,128)(2,1)} %bitcast.9, ...), custom_call_target="tpu_custom_call" | custom-call | tf_op jit(solution)/shard_map/exchange/pallas_call | solution.py:414
  89.6 7.6 %finish.1 = (bf16[8,32,8192]{2,1,0:T(8,128)(2,1)}, f32[8,32,1024]{2,1,0:T(8,128)}, bf16[1,4,8,32,8192]{4,3,2,1,0:T(8,128)(2,1)}) custom-call(s32[1]{0:T(128)S(6)} %copy.8.frag, bf16[4,8,32,8192]{3,2,1,0:T(8,128)(2,1)S(1)} %get-tuple-element.10.inner_v, bf16[16,2,2,32,640]{4,3,2,1,0:T(8,128)(2,1)S(1)} %get-tuple-element.11.res_a, ...), custom_call_target="tpu_custom_call" | custom-call | tf_op jit(solution)/shard_map/finish/pallas_call | solution.py:437

commit v4 on v3

--- a/solution.py
+++ b/solution.py
@@ -240,7 +240,6 @@
     for copy in loads(0, 0):
         copy.start()
     mom_copy = pltpu.make_async_copy(momentum, mom, msem)
-    mom_copy.start()
 
     barrier = pltpu.get_barrier_semaphore()
     count = 0
@@ -310,6 +309,7 @@
         return carry
 
     round_chunk(0, 0)
+    mom_copy.start()
     pl.semaphore_wait(barrier, count)
     ticks = pl.cdiv(total + last, 2)
 

time: 97.4 us -> 96.9 us (level)
  no operation moved by 1% of the time
where the time goes in v4:
time: 96.9 us; the launch traced here: 96.7 us
  Pallas kernels  95.4 us (98%)
  between operations  1.29 us (1%)
    pallas_call x1, Pallas kernels, body(): pl.pallas_call(functools.partial(exchange_kernel, (outer, inner_n, chunks...  87.8 us
    pallas_call x1, Pallas kernels, body(): pl.pallas_call(finish_kernel, in_specs=[in_smem] + [in_vmem] * 4, out_spe...  7.57 us

profile of v4, /device:TPU:0, one launch (start us, length us, event | category | flops | bytes accessed | tf_op | source)
XLA Modules:
  0.0 96.7 jit_solution(13460286987830031334)
XLA Ops:
  1.3 87.8 %exchange.1 = (bf16[4,8,32,8192]{3,2,1,0:T(8,128)(2,1)S(1)}, bf16[16,2,2,32,640]{4,3,2,1,0:T(8,128)(2,1)S(1)}, bf16[16,2,2,32,384]{4,3,2,1,0:T(8,128)(2,1)S(1)}, f32[8,32,1024]{2,1,0:T(8,128)S(1)}) custom-call(s32[1]{0:T(128)S(6)} %copy.8.frag, bf16[1,4,8,32,8192]{4,3,2,1,0:T(8,128)(2,1)} %bitcast.7, bf16[8,32,8192]{2,1,0:T(8,128)(2,1)} %bitcast.9, ...), custom_call_target="tpu_custom_call" | custom-call | tf_op jit(solution)/shard_map/exchange/pallas_call | solution.py:414
  89.1 7.6 %finish.1 = (bf16[8,32,8192]{2,1,0:T(8,128)(2,1)}, f32[8,32,1024]{2,1,0:T(8,128)}, bf16[1,4,8,32,8192]{4,3,2,1,0:T(8,128)(2,1)}) custom-call(s32[1]{0:T(128)S(6)} %copy.8.frag, bf16[4,8,32,8192]{3,2,1,0:T(8,128)(2,1)S(1)} %get-tuple-element.10.inner_v, bf16[16,2,2,32,640]{4,3,2,1,0:T(8,128)(2,1)S(1)} %get-tuple-element.11.res_a, ...), custom_call_target="tpu_custom_call" | custom-call | tf_op jit(solution)/shard_map/finish/pallas_call | solution.py:437
